TPU v7x, 128 devices: a whole 4x4x4 slice. The times are simulated.
128 devices in a mesh: rows: 16 (over y, x), cols: 8 (over z, core).
Axes of the slice: x: 4, y: 4, z: 4, core: 2. Of those that a mesh axis runs over, the one named last changes fastest.
Arguments:
- affiliations: float32 [131072, 512], P(('rows', 'cols')), as said below
- tile_block: int32 [128, 240], P(('rows', 'cols')), may hold values from 0 to 1023, as said below
- tile_target: int32 [128, 240], P(('rows', 'cols')), may hold values from 0 to 7
- tile_pattern: int32 [128, 240], P(('rows', 'cols')), may hold values from 0 to 191
- tile_count: int32 [128], P(('rows', 'cols')), may hold values from 15 to 240, as said below
- block_home: int32 [1024], replicated, may hold values from 0 to 1023, as said below
- patterns: int32 [192, 5, 128], replicated, may hold values from 0 to 1073741823, as said below
Outputs:
- updated_affiliations: float32 [131072, 512], P(('rows', 'cols'))
Inputs may be any that keep to these rules, and one draw needn't show every extreme that they name: Live tiles of a device are the first tile_count of its slots, in order of their neighbour's owner row (storage block // 64); some device has exactly 240. `tile_block`: A live tile's neighbour is stored on a device of the same cols index and another rows index; a device's live tiles name at most 4 distinct blocks of one owner row, and in every draw some device names exactly 4 of every other owner row; a (target, neighbour) pair is live at most once on a device; slots past the count hold valid block numbers. `block_home`: A permutation of the node blocks. `patterns`: bits at rows 128 and beyond are zero. `affiliations`: Positive.
All inputs are finite; a program needn't handle non-finite values.
Results may differ from a plain program's by a relative error of at most 0.0003.
Values may be sent and summed in bfloat16 or wider, within the bound.
No kernel may reach another device: no remote copies, remote signals or barrier semaphores. Data moves between devices by JAX's collectives and lax.ppermute only.
A program may use at most 192 MiB of HBM per device.

v0:
```python
import functools

import jax
import jax.numpy as jnp
from jax import lax
from jax.sharding import Mesh
from jax.sharding import PartitionSpec as P

C = 512
BLOCK = 128
LINKS = 4
STEPS = 2
ROWS = ("rows_0", "rows_1")
COLS = ("cols_0", "cols_1")
ROWS_COLS = ("rows_0", "rows_1", "cols_0", "cols_1")


floor_value = 0.001
batch_tiles = 16


def by_axis(x, axes):
    return functools.reduce(lax.psum, axes, x)


def unpack_masks(packed):
    shifts = jnp.arange(30, dtype=jnp.int32)
    bit_values = jnp.right_shift(packed[:, :, None, :], shifts[None, None, :, None]) & 1
    bit_values = bit_values.reshape(packed.shape[0], packed.shape[1] * 30, packed.shape[2])
    return bit_values[:, :BLOCK, :].astype(jnp.float32)


def tile_terms(own_rows, remote_rows, tile_masks, inner_unit):
    scores = (
        jnp.einsum("tnc,tmc->tnm", own_rows, remote_rows, preferred_element_type=jnp.float32)
        / inner_unit
    )
    weights = (tile_masks / (1.0 - jnp.exp(-jnp.maximum(scores, floor_value)))).astype(jnp.bfloat16)
    return jnp.einsum("tnm,tmc->tnc", weights, remote_rows, preferred_element_type=jnp.float32)


def pick_blocks(table, indices):
    slots = jnp.arange(table.shape[0], dtype=jnp.int32)
    selector = (indices[:, None] == slots[None, :]).astype(jnp.bfloat16)
    return jnp.einsum("ts,snc->tnc", selector, table, preferred_element_type=jnp.float32).astype(
        jnp.bfloat16
    )


def run_tiles(
    running,
    start_tile,
    stop_tile,
    own_blocks,
    targets,
    pattern_ids,
    patterns,
    source,
    source_index,
    in_source,
    inner_unit,
):
    turn_count = (stop_tile - start_tile + batch_tiles - 1) // batch_tiles
    offsets = jnp.arange(batch_tiles, dtype=jnp.int32)
    top_tile = targets.shape[0] - 1
    held_ids = jnp.arange(own_blocks.shape[0], dtype=jnp.int32)

    def one_turn(turn_index, partial_sum):
        positions = start_tile + turn_index * batch_tiles + offsets
        live_tiles = positions < stop_tile
        positions = jnp.minimum(positions, top_tile)
        live_tiles = live_tiles & in_source[positions]
        tile_targets = targets[positions]
        own_rows = pick_blocks(own_blocks, tile_targets)
        remote_rows = pick_blocks(source, source_index[positions])
        tile_masks = unpack_masks(patterns[pattern_ids[positions]])
        contribs = tile_terms(own_rows, remote_rows, tile_masks, inner_unit)
        places = ((tile_targets[:, None] == held_ids[None, :]) & live_tiles[:, None]).astype(
            jnp.float32
        )
        return partial_sum + jnp.einsum(
            "tb,tnc->bnc", places, contribs, precision=lax.Precision.HIGHEST
        )

    return lax.fori_loop(0, turn_count, one_turn, running)


def per_device(
    affiliations, tile_block, tile_target, tile_pattern, tile_count, block_home, patterns
):
    row_count = lax.axis_size(ROWS)
    col_count = lax.axis_size(COLS)
    blocks_held = affiliations.shape[0] // BLOCK
    inner_unit = 192 * C * col_count * blocks_held // LINKS
    step_amount = 0.3 / (affiliations.shape[0] * row_count * col_count)
    block_ids = tile_block[0]
    targets = tile_target[0]
    pattern_ids = tile_pattern[0]
    active_count = tile_count[0]
    cap_tiles = block_ids.shape[0]
    home_slots = block_home[block_ids]
    owners = home_slots // (col_count * blocks_held)
    j_local = home_slots % blocks_held
    active = jnp.arange(cap_tiles, dtype=jnp.int32) < active_count
    owner_hits = (owners[:, None] == jnp.arange(row_count, dtype=jnp.int32)[None, :]) & active[
        :, None
    ]
    all_tiles = jnp.ones((cap_tiles,), dtype=bool)
    empty_sum = jnp.zeros((blocks_held, BLOCK, C), jnp.float32)
    peer_cap = blocks_held // 2
    local_hits = j_local[:, None] == jnp.arange(blocks_held, dtype=jnp.int32)[None, :]
    wanted = jnp.dot(owner_hits.astype(jnp.int32).T, local_hits.astype(jnp.int32)) > 0
    request_rank = jnp.cumsum(wanted.astype(jnp.int32), axis=1) - 1
    chosen = wanted[:, None, :] & (
        request_rank[:, None, :] == jnp.arange(peer_cap, dtype=jnp.int32)[None, :, None]
    )
    requests = jnp.sum(
        chosen.astype(jnp.int32) * jnp.arange(blocks_held, dtype=jnp.int32)[None, None, :], axis=2
    )
    incoming = lax.all_to_all(requests, ROWS, split_axis=0, concat_axis=0, tiled=True)
    source_index = owners * peer_cap + request_rank[owners, j_local]
    current = affiliations
    for step_number in range(STEPS):
        col_sums = by_axis(jnp.sum(current, axis=0), ROWS_COLS)
        own_blocks = current.astype(jnp.bfloat16).reshape(blocks_held, BLOCK, C)
        outgoing = own_blocks[incoming]
        fetched = lax.all_to_all(outgoing, ROWS, split_axis=0, concat_axis=0, tiled=True)
        fetched = fetched.reshape(row_count * peer_cap, BLOCK, C)
        neighbour = run_tiles(
            empty_sum,
            0,
            active_count,
            own_blocks,
            targets,
            pattern_ids,
            patterns,
            fetched,
            source_index,
            all_tiles,
            inner_unit,
        )
        gradient = neighbour.reshape(current.shape) - col_sums[None, :]
        current = jnp.maximum(current + step_amount * gradient, 0.0)
    return current


def solution(mesh):
    torus = Mesh(mesh.devices.reshape(4, 4, 4, 2), ("rows_0", "rows_1", "cols_0", "cols_1"))
    return jax.shard_map(
        per_device,
        mesh=torus,
        in_specs=(
            P(ROWS_COLS, None),
            P(ROWS_COLS, None),
            P(ROWS_COLS, None),
            P(ROWS_COLS, None),
            P(ROWS_COLS),
            P(),
            P(),
        ),
        out_specs=P(ROWS_COLS, None),
        check_vma=False,
    )
```

profile of v0, /device:TPU:56, one launch (start us, length us, event | category | flops | bytes accessed | tf_op | source)
XLA Modules:
  0.0 1189.4 jit_solution(9869656308941866640)
XLA Ops:
  3.8 7.2 all-to-all-start
  16.8 5.4 gather_fusion.12
  22.1 11.0 copy.123
  33.2 6.7 all-to-all-start.1
  43.7 76.5 %psum.56 = f32[512]{0:T(512)S(1)} all-reduce(f32[512]{0:T(512)S(1)} %get-tuple-element.324), channel_id=1, replica_groups=mesh['rows_0'=4,'rows_1'=4,'cols_0'=4,'cols_1'=2] {'rows_0'}, use_global_device_ids=true, to_apply=%region_5.6 | all-reduce | flops 512 | bytes 4096 | tf_op jit(solution)/shard_map/psum | solution.py:23
  120.3 41.1 %psum.57 = f32[512]{0:T(512)S(1)} all-reduce(f32[512]{0:T(512)S(1)} %psum.56), channel_id=1, replica_groups=mesh['rows_0'=4,'rows_1'=4,'cols_0'=4,'cols_1'=2] {'rows_1'}, use_global_device_ids=true, to_apply=%region_6.7 | all-reduce | flops 512 | bytes 4096 | tf_op jit(solution)/shard_map/psum | solution.py:23
  161.4 9.0 psum.58
  173.0 9.1 copy.124
  182.1 11.3 copy.127
  195.0 432.6 %while.22 = (s32[]{:T(128)}, f32[8,128,512]{2,0,1:T(8,128)}, s32[]{:T(128)}, s32[240]{0:T(256)S(1)}, s32[]{:T(128)}, /*index=5*/s32[240]{0:T(256)S(1)}, s32[192,...) while((s32[]{:T(128)}, f32[8,128,512]{2,0,1:T(8,128)}, ...), condition=%wide.region_3.4_spmd.clone, body=%wide.region_2.3_spmd.clone.sunk | while | flops 793513536 | bytes 46535636 | solution.py:85
  215.8 8.0 fusion.146
  244.6 8.0 fusion.146
  253.4 4.6 convolution_convert_fusion.8
  273.4 8.0 fusion.146
  302.3 8.0 fusion.146
  311.0 4.6 convolution_convert_fusion.8
  331.1 8.0 fusion.146
  359.9 8.0 fusion.146
  368.6 4.6 convolution_convert_fusion.8
  388.7 8.0 fusion.146
  417.5 8.0 fusion.146
  446.3 8.0 fusion.146
  455.0 4.6 convolution_convert_fusion.8
  475.1 8.0 fusion.146
  503.9 8.0 fusion.146
  512.7 4.6 convolution_convert_fusion.8
  532.8 8.0 fusion.146
  561.6 8.0 fusion.146
  570.3 4.6 convolution_convert_fusion.8
  590.4 8.0 fusion.146
  619.2 8.0 fusion.146
  632.6 5.4 gather_fusion.13
  638.0 11.0 copy.129
  649.1 4.7 all-to-all-start.2
  654.3 27.7 %psum.60 = f32[512]{0:T(512)S(1)} all-reduce(f32[512]{0:T(512)S(1)} %get-tuple-element.321), channel_id=1, replica_groups=mesh['rows_0'=4,'rows_1'=4,'cols_0'=4,'cols_1'=2] {'rows_0'}, use_global_device_ids=true, to_apply=%region_12.13 | all-reduce | flops 512 | bytes 4096 | tf_op jit(solution)/shard_map/psum | solution.py:23
  682.0 38.4 %psum.61 = f32[512]{0:T(512)S(1)} all-reduce(f32[512]{0:T(512)S(1)} %psum.60), channel_id=1, replica_groups=mesh['rows_0'=4,'rows_1'=4,'cols_0'=4,'cols_1'=2] {'rows_1'}, use_global_device_ids=true, to_apply=%region_13.14 | all-reduce | flops 512 | bytes 4096 | tf_op jit(solution)/shard_map/psum | solution.py:23
  720.4 6.5 psum.62
  729.5 9.1 copy.130
  738.6 11.3 copy.133
  751.6 432.8 %while.23 = (s32[]{:T(128)}, f32[8,128,512]{2,0,1:T(8,128)}, s32[]{:T(128)}, s32[240]{0:T(256)S(1)}, s32[]{:T(128)}, /*index=5*/s32[240]{0:T(256)S(1)}, s32[192,...) while((s32[]{:T(128)}, f32[8,128,512]{2,0,1:T(8,128)}, ...), condition=%wide.region_10.11_spmd.clone, body=%wide.region_9.10_spmd.clone.sunk | while | flops 793513536 | bytes 46535636 | solution.py:85
  752.3 4.6 convolution_convert_fusion.10
  772.4 8.1 fusion.162
  781.1 4.6 convolution_convert_fusion.10
  801.2 8.1 fusion.162
  830.1 8.1 fusion.162
  838.8 4.6 convolution_convert_fusion.10
  858.9 8.1 fusion.162
  867.7 4.6 convolution_convert_fusion.10
  887.8 8.1 fusion.162
  896.5 4.6 convolution_convert_fusion.10
  916.6 8.1 fusion.162
  945.5 8.1 fusion.162
  954.2 4.6 convolution_convert_fusion.10
  974.3 8.1 fusion.162
  983.1 4.6 convolution_convert_fusion.10
  1003.2 8.1 fusion.162
  1032.0 8.1 fusion.162
  1060.9 8.1 fusion.162
  1069.6 4.6 convolution_convert_fusion.10
  1089.7 8.1 fusion.162
  1098.5 4.6 convolution_convert_fusion.10
  1118.6 8.1 fusion.162
  1147.4 8.1 fusion.162
  1176.3 8.1 fusion.162
  (785 shorter events, 583.0 us)
Async XLA Ops:
  3.8 12.7 %all-to-all-start = ((s32[16,1,4]{2,1,0:T(1,128)}), s32[16,1,4]{2,1,0:T(1,128)S(1)}, u32[]{:S(2)}, u32[]{:S(2)}) async-start(s32[16,1,4]{2,1,0:T(1,128)} %copy.120), calls=%async_computation | async-start | bytes 16384 | tf_op jit(solution)/shard_map/all_to_all | solution.py:120
  33.2 139.9 %all-to-all-start.1 = ((bf16[16,4,128,512]{3,1,2,0:T(4,128)(2,1)}), bf16[16,4,128,512]{3,1,2,0:T(4,128)(2,1)}, u32[]{:S(2)}, u32[]{:S(2)}) async-start(bf16[16,4,128,512]{3,1,2,0:T(4,128)(2,1)} %copy.123), calls=%async_computation.1 | async-start | bytes 16777216 | tf_op jit(solution)/shard_map/all_to_all | solution.py:127
  195.0 6.0 copy-start.4
  215.8 8.0 copy-start.5
  223.8 6.0 copy-start.4
  244.6 8.0 copy-start.5
  252.7 6.0 copy-start.4
  273.4 8.0 copy-start.5
  281.5 6.0 copy-start.4
  302.2 8.0 copy-start.5
  310.3 6.0 copy-start.4
  331.1 8.0 copy-start.5
  339.1 6.0 copy-start.4
  359.9 8.0 copy-start.5
  367.9 6.0 copy-start.4
  388.7 8.0 copy-start.5
  396.7 6.0 copy-start.4
  417.5 8.0 copy-start.5
  425.5 6.0 copy-start.4
  446.3 8.0 copy-start.5
  454.4 6.0 copy-start.4
  475.1 8.0 copy-start.5
  483.2 6.0 copy-start.4
  503.9 8.0 copy-start.5
  512.0 6.0 copy-start.4
  532.7 8.0 copy-start.5
  540.8 6.0 copy-start.4
  561.6 8.0 copy-start.5
  569.6 6.0 copy-start.4
  590.4 8.0 copy-start.5
  598.4 6.0 copy-start.4
  619.2 8.0 copy-start.5
  649.1 80.5 %all-to-all-start.2 = ((bf16[16,4,128,512]{3,1,2,0:T(4,128)(2,1)}), bf16[16,4,128,512]{3,1,2,0:T(4,128)(2,1)}, u32[]{:S(2)}, u32[]{:S(2)}) async-start(bf16[16,4,128,512]{3,1,2,0:T(4,128)(2,1)} %copy.129), calls=%async_computation.2 | async-start | bytes 16777216 | tf_op jit(solution)/shard_map/all_to_all | solution.py:127
  751.6 6.0 copy-start.6
  772.3 8.1 copy-start.7
  780.4 6.0 copy-start.6
  801.2 8.1 copy-start.7
  809.3 6.0 copy-start.6
  830.1 8.1 copy-start.7
  838.1 6.0 copy-start.6
  858.9 8.1 copy-start.7
  867.0 6.0 copy-start.6
  887.8 8.1 copy-start.7
  895.8 6.0 copy-start.6
  916.6 8.1 copy-start.7
  924.7 6.0 copy-start.6
  945.5 8.1 copy-start.7
  953.5 6.0 copy-start.6
  974.3 8.1 copy-start.7
  982.4 6.0 copy-start.6
  1003.2 8.1 copy-start.7
  1011.3 6.0 copy-start.6
  1032.0 8.1 copy-start.7
  1040.1 6.0 copy-start.6
  1060.9 8.1 copy-start.7
  1069.0 6.0 copy-start.6
  1089.7 8.1 copy-start.7
  1097.8 6.0 copy-start.6
  1118.6 8.1 copy-start.7
  1126.7 6.0 copy-start.6
  1147.4 8.1 copy-start.7
  1155.5 6.0 copy-start.6
  1176.3 8.1 copy-start.7
  1184.4 4.8 copy-start.1
  (7 other events, 14.5 us)
where the time goes:
time: 1200 us; the launch traced here: 1190 us
  matrix products  642 us (54%)
  local copies, waits for them, and re-layouts  227 us (19%)
  blocking collectives  205 us (17%)
  other arithmetic  90.4 us (8%)
  starting transfers between devices  18.5 us (2%)
    dot_general x30, matrix products, one_turn(): jnp.einsum('tb,tnc->bnc', places, contribs, precision=lax.Precision.HIGHEST)  242 us
    psum x8, blocking collectives, by_axis(): return functools.reduce(lax.psum, axes, x)  205 us
    dot_general x60, matrix products, pick_blocks(): jnp.einsum('ts,snc->tnc', selector, table, preferred_element_type=jnp.flo...  162 us
    dot_general x30, matrix products, tile_terms(): jnp.einsum('tnm,tmc->tnc', weights, remote_rows, preferred_element_type=j...  136 us
    dot_general x30, matrix products, tile_terms(): jnp.einsum('tnc,tmc->tnm', own_rows, remote_rows, preferred_element_type=...  102 us
    gather x90, local copies, waits for them, and re-layouts, one_turn(): tile_masks = unpack_masks(patterns[pattern_ids[positions]])  70.9 us
    convert_element_type x30, other arithmetic, tile_terms(): (tile_masks / (1.0 - jnp.exp(-jnp.maximum(scores, floor_value)))).astype(...  63.8 us
    gather x4, local copies, waits for them, and re-layouts, per_device(): outgoing = own_blocks[incoming]  32.8 us
  transfers between devices with their start and end apart: 3, of which 1 were waited for; matrix products, arithmetic and copies ran while one was open for 1% of the time, Pallas kernels for 0%

commit v1 on v0

v1 whole, which is shorter than its diff:
```python
import functools

import jax
import jax.numpy as jnp
from jax import lax
from jax.experimental import pallas as pl
from jax.experimental.pallas import tpu as pltpu
from jax.sharding import Mesh
from jax.sharding import PartitionSpec as P

C = 512
BLOCK = 128
STEPS = 2
BPD = 8
SIDE = 4
CAP = 4
N_COLS = 8
NODES = 131072
UNIT = 1572864
PATTERNS = 192
TILES = 240
GROUP = 2
PHASES = 3
KEYS = PHASES * BPD
GROUPS = (TILES + KEYS * (GROUP - 1)) // GROUP + 2 * PHASES
SLOTS = GROUPS * GROUP
FLOOR = 0.001
STEP_SIZE = 0.3 / NODES

ALL = ("rows_0", "rows_1", "cols_0", "cols_1")
VMEM = pl.BlockSpec(memory_space=pltpu.VMEM)
SMEM = pl.BlockSpec(memory_space=pltpu.SMEM)
ANY = pl.BlockSpec(memory_space=pl.ANY)


def pairs(first, second):
    out = []
    for y in range(SIDE):
        for x in range(SIDE):
            for z in range(4):
                for core in range(2):
                    dx, dy = (first, second) if core == 0 else (second, first)
                    sy, sx = (y + dy) % SIDE, (x + dx) % SIDE
                    out.append((((sy * 4 + sx) * 4 + z) * 2 + core, ((y * 4 + x) * 4 + z) * 2 + core))
    return out


def fetch(value, first, second):
    return lax.ppermute(value, ALL, pairs(first, second))


def sum_over_mesh(part):
    for axis, size in (("cols_1", 2), ("cols_0", 4), ("rows_1", 4), ("rows_0", 4)):
        step = 1
        while step < size:
            part = part + lax.ppermute(part, axis, [(i, i ^ step) for i in range(size)])
            step *= 2
    return part


def plan_kernel(
    place, blocks, targets, pattern_ids, count, home,
    requests, sources, patterns, group_target, phase_start,
    rank, fill, tile_source, tile_key, per_key, cursor,
):
    first, second, core = place[0], place[1], place[2]
    live = count[0]

    def clear(ref, size, value):
        def body(i, _):
            ref[i] = value
            return 0

        lax.fori_loop(0, size, body, 0)

    clear(rank, 128, -1)
    clear(fill, 16, 0)
    clear(requests, 64, 0)
    clear(per_key, KEYS, 0)
    clear(sources, SLOTS, 0)
    clear(patterns, SLOTS, PATTERNS)
    clear(group_target, GROUPS, 0)

    def note(t, _):
        slot = home[blocks[t]]
        row = slot // (N_COLS * BPD)
        local = slot & (BPD - 1)
        y, x = row // SIDE, row & (SIDE - 1)
        owner_first = jnp.where(core == 0, x, y)
        owner_second = jnp.where(core == 0, y, x)
        k = (owner_first - first) & (SIDE - 1)
        m = (owner_second - second) & (SIDE - 1)
        pair = m * SIDE + k
        seen = rank[pair * BPD + local]
        held = fill[pair]
        mine = jnp.where(seen < 0, held, seen)
        mine = jnp.minimum(mine, CAP - 1)
        rank[pair * BPD + local] = mine
        fill[pair] = jnp.where(seen < 0, held + 1, held)
        requests[pair * CAP + mine] = local
        whole = jnp.maximum(k - 1, 0) * BPD + local
        picked = k * CAP + mine + jnp.where(m == 3, SIDE * CAP, 0)
        tile_source[t] = jnp.where(m == 0, whole, picked)
        phase = jnp.where(m == 0, 0, jnp.where(m == 2, 2, 1))
        key = phase * BPD + targets[t]
        tile_key[t] = key
        per_key[key] = per_key[key] + 1
        return 0

    lax.fori_loop(0, live, note, 0)

    base = jnp.int32(0)
    for phase in range(PHASES):
        phase_start[phase] = base
        top = base
        for target in range(BPD):
            key = phase * BPD + target
            size = (per_key[key] + GROUP - 1) // GROUP
            cursor[key] = top * GROUP
            top = top + size
        used = top - base
        base = base + jnp.maximum(2, (used + 1) // 2 * 2)
    phase_start[PHASES] = base

    def put(t, _):
        key = tile_key[t]
        at = cursor[key]
        cursor[key] = at + 1
        sources[at] = tile_source[t]
        patterns[at] = pattern_ids[t]
        group_target[at // GROUP] = targets[t]
        return 0

    lax.fori_loop(0, live, put, 0)


def make_plan(place, blocks, targets, pattern_ids, count, home):
    i32 = jnp.int32
    return pl.pallas_call(
        plan_kernel,
        out_shape=(
            jax.ShapeDtypeStruct((64,), i32),
            jax.ShapeDtypeStruct((SLOTS,), i32),
            jax.ShapeDtypeStruct((SLOTS,), i32),
            jax.ShapeDtypeStruct((GROUPS,), i32),
            jax.ShapeDtypeStruct((PHASES + 1,), i32),
        ),
        in_specs=[SMEM] * 6,
        out_specs=(SMEM,) * 5,
        scratch_shapes=[
            pltpu.SMEM((128,), i32),
            pltpu.SMEM((16,), i32),
            pltpu.SMEM((TILES,), i32),
            pltpu.SMEM((TILES,), i32),
            pltpu.SMEM((KEYS,), i32),
            pltpu.SMEM((KEYS,), i32),
        ],
        name="plan",
    )(place, blocks, targets, pattern_ids, count, home)


def pick_kernel(asked, own, far1, far2, far3, out1, out2, out3, sems):
    copies = []
    for m, out in enumerate((out1, out2, out3)):
        for k, table in enumerate((own, far1, far2, far3)):
            for r in range(CAP):
                local = asked[m, k * CAP + r]
                copies.append(
                    pltpu.make_async_copy(
                        table.at[local], out.at[k * CAP + r], sems.at[len(copies)]
                    )
                )
    for copy in copies:
        copy.start()
    for copy in copies:
        copy.wait()


def pick(asked, own, far):
    shape = jax.ShapeDtypeStruct((SIDE * CAP, BLOCK, C), jnp.bfloat16)
    return pl.pallas_call(
        pick_kernel,
        out_shape=(shape,) * 3,
        in_specs=[SMEM] + [ANY] * 4,
        out_specs=(ANY,) * 3,
        scratch_shapes=[pltpu.SemaphoreType.DMA((3 * SIDE * CAP,))],
        name="pick",
    )(asked, own, *far)


def tile_kernel(phase, parts, step_kind, *refs):
    refs = list(refs)
    sources, pattern_ids, group_target, phase_start = refs[:4]
    words, own = refs[4:6]
    tables = refs[6 : 6 + parts]
    refs = refs[6 + parts :]
    last = phase == PHASES - 1
    if phase > 0:
        earlier = refs.pop(0)
    if last:
        current, col_sums = refs.pop(0), refs.pop(0)
        fresh = refs.pop(0)
        if step_kind == "more":
            rounded, part_sums = refs.pop(0), refs.pop(0)
        total = None
    else:
        total = refs.pop(0)
    if last:
        total = refs.pop(0)
    held, score_a, score_b, bits, sems = refs

    copies = []
    at = 0
    for i, table in enumerate(tables):
        n = table.shape[0]
        copies.append(pltpu.make_async_copy(table, held.at[pl.ds(at, n)], sems.at[i]))
        at += n
    for copy in copies:
        copy.start()
    row = lax.broadcasted_iota(jnp.int32, (BLOCK, BLOCK), 0)
    bits[...] = lax.shift_left(jnp.ones_like(row), lax.rem(row, 30))
    if phase > 0:
        total[...] = earlier[...]
    else:
        total[...] = jnp.zeros_like(total)
    for copy in copies:
        copy.wait()

    sub = lax.broadcasted_iota(jnp.int32, (8, BLOCK), 0)

    def word_rows(pattern):
        rows = []
        for v in range(BLOCK // 8):
            low, high = 8 * v // 30, (8 * v + 7) // 30
            chunk = jnp.broadcast_to(words[pattern, low : low + 1, :], (8, BLOCK))
            if high != low:
                other = jnp.broadcast_to(words[pattern, high : high + 1, :], (8, BLOCK))
                chunk = jnp.where(sub + 8 * v < 30 * high, chunk, other)
            rows.append(chunk)
        return jnp.concatenate(rows, axis=0)

    def remote(group):
        return jnp.concatenate([held[sources[group * GROUP + i]] for i in range(GROUP)], axis=0)

    def score(group, out):
        mine = own[group_target[group]]
        out[...] = lax.dot_general(
            mine, remote(group), (((1,), (1,)), ((), ())), preferred_element_type=jnp.float32
        )

    def add(group, scores):
        weights = []
        for i in range(GROUP):
            packed = word_rows(pattern_ids[group * GROUP + i])
            negative = jnp.minimum(scores[:, i * BLOCK : (i + 1) * BLOCK] * (-1.0 / UNIT), -FLOOR)
            weight = 1.0 / (1.0 - jnp.exp(negative))
            linked = (packed & bits[...]) != 0
            weights.append(jnp.where(linked, weight, 0.0).astype(jnp.bfloat16))
        target = group_target[group]
        total[target] += jnp.dot(
            jnp.concatenate(weights, axis=1), remote(group), preferred_element_type=jnp.float32
        )

    start, stop = phase_start[phase], phase_start[phase + 1]
    score(start, score_a)

    def two(i, _):
        group = start + 2 * i
        score(group + 1, score_b)
        add(group, score_a)
        score(jnp.minimum(group + 2, stop - 1), score_a)
        add(group + 1, score_b)
        return 0

    lax.fori_loop(0, (stop - start) // 2, two, 0)

    if last:
        sums = jnp.sum(col_sums[...], axis=0, keepdims=True)
        parts_sum = jnp.zeros((8, C), jnp.float32)
        for j in range(BPD):
            moved = current[j] + STEP_SIZE * (total[j] - sums)
            moved = jnp.maximum(moved, 0.0)
            fresh[j] = moved
            if step_kind == "more":
                rounded[j] = moved.astype(jnp.bfloat16)
                parts_sum = parts_sum + jnp.sum(moved.reshape(BLOCK // 8, 8, C), axis=0)
        if step_kind == "more":
            part_sums[...] = parts_sum


def run_tiles(phase, lists, words, own, tables, earlier=None, current=None, col_sums=None, more=True):
    f32 = jnp.float32
    blocks = jax.ShapeDtypeStruct((BPD, BLOCK, C), f32)
    args = [*lists, words, own, *tables]
    specs = [SMEM] * 4 + [VMEM] * 2 + [ANY] * len(tables)
    scratch = []
    if phase > 0:
        args.append(earlier)
        specs.append(VMEM)
    if phase == PHASES - 1:
        args += [current, col_sums]
        specs += [VMEM, VMEM]
        out = [blocks]
        if more:
            out += [
                jax.ShapeDtypeStruct((BPD, BLOCK, C), jnp.bfloat16),
                jax.ShapeDtypeStruct((8, C), f32),
            ]
        scratch.append(pltpu.VMEM((BPD, BLOCK, C), f32))
    else:
        out = [blocks]
    rows = sum(t.shape[0] for t in tables)
    scratch += [
        pltpu.VMEM((rows, BLOCK, C), jnp.bfloat16),
        pltpu.VMEM((BLOCK, GROUP * BLOCK), f32),
        pltpu.VMEM((BLOCK, GROUP * BLOCK), f32),
        pltpu.VMEM((BLOCK, BLOCK), jnp.int32),
        pltpu.SemaphoreType.DMA((len(tables),)),
    ]
    return pl.pallas_call(
        functools.partial(tile_kernel, phase, len(tables), "more" if more else "end"),
        out_shape=tuple(out),
        in_specs=specs,
        out_specs=(VMEM,) * len(out),
        scratch_shapes=scratch,
        compiler_params=pltpu.CompilerParams(vmem_limit_bytes=48 << 20),
        name="tiles%d" % phase,
    )(*args)


def per_device(affiliations, tile_block, tile_target, tile_pattern, tile_count, block_home, patterns):
    y, x = lax.axis_index("rows_0"), lax.axis_index("rows_1")
    core = lax.axis_index("cols_1")
    first = jnp.where(core == 0, x, y)
    second = jnp.where(core == 0, y, x)
    place = jnp.stack([first, second, core]).astype(jnp.int32)
    requests, *lists = make_plan(
        place, tile_block[0], tile_target[0], tile_pattern[0], tile_count, block_home
    )
    requests = requests.reshape(SIDE, SIDE * CAP)
    asked = jnp.stack([fetch(requests[m], 0, SIDE - m) for m in (1, 2, 3)])
    words = jnp.concatenate([patterns, jnp.zeros((1, *patterns.shape[1:]), jnp.int32)], axis=0)

    current = affiliations.reshape(BPD, BLOCK, C)
    own = current.astype(jnp.bfloat16)
    part = jnp.sum(affiliations.reshape(BPD * BLOCK // 8, 8, C), axis=0)
    for step in range(STEPS):
        far1, far3, far2 = fetch(own, 1, 0), fetch(own, 3, 0), fetch(own, 2, 0)
        col_sums = sum_over_mesh(part)
        out1, out2, out3 = pick(asked, own, (far1, far2, far3))
        side1, side3, side2 = fetch(out1, 0, 1), fetch(out3, 0, 3), fetch(out2, 0, 2)
        (total,) = run_tiles(0, lists, words, own, (far1, far2, far3))
        (total,) = run_tiles(1, lists, words, own, (side1, side3), total)
        more = step < STEPS - 1
        out = run_tiles(2, lists, words, own, (side2,), total, current, col_sums, more)
        if more:
            current, own, part = out
        else:
            (current,) = out
    return current.reshape(affiliations.shape)


def solution(mesh):
    torus = Mesh(mesh.devices.reshape(4, 4, 4, 2), ALL)
    return jax.shard_map(
        per_device,
        mesh=torus,
        in_specs=(P(ALL, None), P(ALL, None), P(ALL, None), P(ALL, None), P(ALL), P(), P()),
        out_specs=P(ALL, None),
        check_vma=False,
    )
```

time: 1200 us -> 659 us (0.55)
  the two profiles are of different devices: /device:TPU:56 before, /device:TPU:39 now
where the time goes in v1:
time: 659 us; the launch traced here: 661 us
  Pallas kernels  488 us (74%)
  waiting for transfers between devices  130 us (20%)
  starting transfers between devices  23.5 us (4%)
  local copies, waits for them, and re-layouts  13.9 us (2%)
    pallas_call x2, Pallas kernels, pick(): pl.pallas_call(pick_kernel, out_shape=(shape,) * 3, in_specs=[SMEM] + [AN...  386 us
    ppermute x14, waiting for transfers between devices, sum_over_mesh(): part = part + lax.ppermute(part, axis, [(i, i ^ step) for i in range(size)])  102 us
    pallas_call x6, Pallas kernels, run_tiles(): pl.pallas_call(functools.partial(tile_kernel, phase, len(tables), 'more'...  82.3 us
    ppermute x15, waiting for transfers between devices, fetch(): return lax.ppermute(value, ALL, pairs(first, second))  28.3 us
    pallas_call x1, Pallas kernels, make_plan(): pl.pallas_call(plan_kernel, out_shape=(jax.ShapeDtypeStruct((64,), i32),...  19.9 us
    ppermute x15, starting transfers between devices, fetch(): return lax.ppermute(value, ALL, pairs(first, second))  14.7 us
  transfers between devices with their start and end apart: 29, of which 18 were waited for; matrix products, arithmetic and copies ran while one was open for 1% of the time, Pallas kernels for 12%

profile of v1, /device:TPU:39, one launch (start us, length us, event | category | flops | bytes accessed | tf_op | source)
XLA Modules:
  0.0 661.2 jit_solution(1699512862152985442)
XLA Ops:
  0.0 1.7 convert_element_type.3.own.refs_5_
  1.7 1.4 collective-permute-start.5
  3.1 2.6 collective-permute-start.4
  5.7 1.1 collective-permute-start.3
  7.4 0.6 pad_add_fusion.1.place
  8.1 19.9 %plan.1 = (s32[64]{0:T(128)}, s32[276]{0:T(512)}, s32[276]{0:T(512)}, s32[138]{0:T(256)}, s32[4]{0:T(128)}) custom-call(s32[3]{0:T(128)} %pad_add_fusion.1.place, s32[240]{0:T(256)} %bitcast.15, s32[240]{0:T(256)} %bitcast.16, s32[240]{0:T(256)} %bitcast.17, s32[1]{0:T(128)S(6)} %copy.9.count, s32[1024]{0:T(1024)} %home.1), custom_call_target="tpu_custom_call" | custom-call | tf_op jit(solution)/shard_map/plan/pallas_call | solution.py:139
  27.9 0.8 fusion
  28.8 1.5 collective-permute-start.2
  30.2 0.9 collective-permute-done
  31.2 1.2 collective-permute-done.2
  32.4 2.7 collective-permute-done.1
  35.1 0.6 pad_add_fusion.asked
  35.7 1.0 copy-done.5
  36.6 192.8 %pick.2 = (bf16[16,128,512]{2,1,0:T(8,128)(2,1)}, bf16[16,128,512]{2,1,0:T(8,128)(2,1)}, bf16[16,128,512]{2,1,0:T(8,128)(2,1)}) custom-call(s32[3,16]{1,0:T(4,128)} %pad_add_fusion.asked, bf16[8,128,512]{2,1,0:T(8,128)(2,1)} %copy-done, bf16[8,128,512]{2,1,0:T(8,128)(2,1)} %collective-permute-done.3.far1.refs_6_, ...), custom_call_target="tpu_custom_call" | custom-call | tf_op jit(solution)/shard_map/pick/pallas_call | solution.py:181
  229.5 0.0 copy-start.19
  229.5 0.1 collective-permute-start.7
  229.6 2.7 collective-permute-start.8
  232.2 1.8 bitcast_reduce_fusion
  234.1 0.1 collective-permute-start.9
  234.2 1.2 collective-permute-done.9
  235.4 2.9 collective-permute-done.10
  238.2 2.2 collective-permute-start.11
  240.5 2.2 collective-permute-done.11
  242.6 0.6 collective-permute-start.12
  243.2 34.9 %collective-permute-done.12 = f32[8,512]{1,0:T(8,128)S(1)} collective-permute-done((f32[8,512]{1,0:T(8,128)S(1)}, f32[8,512]{1,0:T(8,128)S(1)}, u32[]{:S(2)}, u32[]{:S(2)}) %collective-permute-start.12) | collective-permute-done | bytes 16416 | tf_op jit(solution)/shard_map/ppermute | solution.py:56
  278.1 2.0 collective-permute-start.13
  280.1 2.1 collective-permute-done.13
  282.2 2.6 collective-permute-done.14
  284.8 0.3 copy.8
  285.1 0.1 concatenate.3.refs_4_
  285.2 3.7 collective-permute-done.15
  288.9 9.9 %tiles0.2.refs_8_ = f32[8,128,512]{2,1,0:T(8,128)} custom-call(s32[276]{0:T(512)S(1)} %copy-done.12, s32[276]{0:T(512)S(1)} %copy-done.13, s32[138]{0:T(256)S(1)} %copy-done.14, s32[4]{0:T(128)S(1)} %copy-done.15, s32[193,5,128]{2,1,0:T(8,128)S(1)} %concatenate.3.refs_4_, bf16[8,128,512]{2,1,0:T(8,128)(2,1)S(1)} %copy-done.1, ...), custom_call_target="tpu_custom_call" | custom-call | tf_op jit(solution)/shard_map/tiles0/pallas_call | solution.py:320
  298.9 0.0 copy-start.17
  298.9 1.3 copy-done.17
  300.2 19.2 %tiles1.2.refs_7_ = f32[8,128,512]{2,1,0:T(8,128)S(1)} custom-call(s32[276]{0:T(512)S(1)} %copy-done.12, s32[276]{0:T(512)S(1)} %copy-done.13, s32[138]{0:T(256)S(1)} %copy-done.14, s32[4]{0:T(128)S(1)} %copy-done.15, s32[193,5,128]{2,1,0:T(8,128)S(1)} %concatenate.3.refs_4_, bf16[8,128,512]{2,1,0:T(8,128)(2,1)S(1)} %copy-done.1, ...), custom_call_target="tpu_custom_call" | custom-call | tf_op jit(solution)/shard_map/tiles1/pallas_call | solution.py:320
  319.4 1.3 copy-done.4
  320.8 1.3 copy-done.16
  322.1 12.5 %tiles2.2 = (f32[8,128,512]{2,1,0:T(8,128)S(1)}, bf16[8,128,512]{2,1,0:T(8,128)(2,1)S(1)}, f32[8,512]{1,0:T(8,128)S(1)}) custom-call(s32[276]{0:T(512)S(1)} %copy-done.12, s32[276]{0:T(512)S(1)} %copy-done.13, s32[138]{0:T(256)S(1)} %copy-done.14, s32[4]{0:T(128)S(1)} %copy-done.15, s32[193,5,128]{2,1,0:T(8,128)S(1)} %concatenate.3.refs_4_, ...), custom_call_target="tpu_custom_call" | custom-call | tf_op jit(solution)/shard_map/tiles2/pallas_call | solution.py:320
  334.6 1.3 copy-done.11
  336.0 2.7 collective-permute-start.16
  338.6 23.4 %collective-permute-done.18.far3.refs_8_ = bf16[8,128,512]{2,1,0:T(8,128)(2,1)S(1)} collective-permute-done((bf16[8,128,512]{2,1,0:T(8,128)(2,1)S(1)}, bf16[8,128,512]{2,1,0:T(8,128)(2,1)S(1)}, u32[]{:S(2)}, u32[]{:S(2)}) %collective-permute-start.18) | collective-permute-done | bytes 1048608 | tf_op jit(solution)/shard_map/ppermute | solution.py:49
  362.1 1.0 copy-done.9
  363.1 0.3 copy-done.7
  363.5 192.8 %pick.3 = (bf16[16,128,512]{2,1,0:T(8,128)(2,1)}, bf16[16,128,512]{2,1,0:T(8,128)(2,1)}, bf16[16,128,512]{2,1,0:T(8,128)(2,1)}) custom-call(s32[3,16]{1,0:T(4,128)} %pad_add_fusion.asked, bf16[8,128,512]{2,1,0:T(8,128)(2,1)} %copy-done.2, bf16[8,128,512]{2,1,0:T(8,128)(2,1)} %collective-permute-done.16.far1.refs_6_, bf16[8,128,512]{2,1,0:T(8,128)(2,1)} %copy-done.9, ...), custom_call_target="tpu_custom_call" | custom-call | tf_op jit(solution)/shard_map/pick/pallas_call | solution.py:181
  556.3 0.1 collective-permute-start.20
  556.4 2.7 collective-permute-start.21
  559.0 1.2 collective-permute-done.22
  560.2 2.9 collective-permute-done.23
  563.1 4.4 collective-permute-done.24
  567.5 0.6 collective-permute-start.25
  568.1 36.5 %collective-permute-done.25 = f32[8,512]{1,0:T(8,128)S(1)} collective-permute-done((f32[8,512]{1,0:T(8,128)S(1)}, f32[8,512]{1,0:T(8,128)S(1)}, u32[]{:S(2)}, u32[]{:S(2)}) %collective-permute-start.25) | collective-permute-done | bytes 16416 | tf_op jit(solution)/shard_map/ppermute | solution.py:56
  604.6 2.3 collective-permute-start.26
  606.9 1.8 collective-permute-done.26
  608.7 2.6 collective-permute-done.27
  611.3 1.1 collective-permute-start.28
  612.4 3.0 collective-permute-done.28
  615.4 1.2 copy-done.3
  616.6 1.2 copy-done.8
  617.8 1.2 copy-done.10
  619.1 9.6 %tiles0.3.refs_8_ = f32[8,128,512]{2,1,0:T(8,128)} custom-call(s32[276]{0:T(512)S(1)} %copy-done.12, s32[276]{0:T(512)S(1)} %copy-done.13, s32[138]{0:T(256)S(1)} %copy-done.14, s32[4]{0:T(128)S(1)} %copy-done.15, s32[193,5,128]{2,1,0:T(8,128)S(1)} %concatenate.3.refs_4_, bf16[8,128,512]{2,1,0:T(8,128)(2,1)S(1)} %copy-done.3, ...), custom_call_target="tpu_custom_call" | custom-call | tf_op jit(solution)/shard_map/tiles0/pallas_call | solution.py:320
  628.7 0.0 copy-start.18
  628.7 1.3 copy-done.18
  630.0 19.2 %tiles1.3.refs_7_ = f32[8,128,512]{2,1,0:T(8,128)S(1)} custom-call(s32[276]{0:T(512)S(1)} %copy-done.12, s32[276]{0:T(512)S(1)} %copy-done.13, s32[138]{0:T(256)S(1)} %copy-done.14, s32[4]{0:T(128)S(1)} %copy-done.15, s32[193,5,128]{2,1,0:T(8,128)S(1)} %concatenate.3.refs_4_, bf16[8,128,512]{2,1,0:T(8,128)(2,1)S(1)} %copy-done.3, ...), custom_call_target="tpu_custom_call" | custom-call | tf_op jit(solution)/shard_map/tiles1/pallas_call | solution.py:320
  649.3 11.8 %tiles2.3 = f32[8,128,512]{2,1,0:T(8,128)} custom-call(s32[276]{0:T(512)S(1)} %copy-done.12, s32[276]{0:T(512)S(1)} %copy-done.13, s32[138]{0:T(256)S(1)} %copy-done.14, s32[4]{0:T(128)S(1)} %copy-done.15, s32[193,5,128]{2,1,0:T(8,128)S(1)} %concatenate.3.refs_4_, bf16[8,128,512]{2,1,0:T(8,128)(2,1)S(1)} %copy-done.3, ...), custom_call_target="tpu_custom_call" | custom-call | tf_op jit(solution)/shard_map/tiles2/pallas_call | solution.py:320
  (64 shorter events, 0.2 us)
Async XLA Ops:
  1.7 34.0 %copy-start = (bf16[8,128,512]{2,1,0:T(8,128)(2,1)}, bf16[8,128,512]{2,1,0:T(8,128)(2,1)S(1)}, u32[]{:S(2)}) copy-start(bf16[8,128,512]{2,1,0:T(8,128)(2,1)S(1)} %convert_element_type.3.own.refs_5_) | copy-start | bytes 3145732
  1.7 33.9 %collective-permute-start.5 = (bf16[8,128,512]{2,1,0:T(8,128)(2,1)S(1)}, bf16[8,128,512]{2,1,0:T(8,128)(2,1)S(1)}, u32[]{:S(2)}, u32[]{:S(2)}) collective-permute-start(bf16[8,128,512]{2,1,0:T(8,128)(2,1)S(1)} %convert_element_type.3.own.refs_5_), channel_id=1, source_target_pairs={{24,0},{97,1},{26,2},{99,3},{28,4},{101,5},{30,6},{103,7},{0,8},{1... | collective-permute-start | bytes 3145736 | tf_op jit(solution)/shard_map/ppermute | solution.py:49
  3.1 32.6 %collective-permute-start.4 = (bf16[8,128,512]{2,1,0:T(8,128)(2,1)S(1)}, bf16[8,128,512]{2,1,0:T(8,128)(2,1)}, u32[]{:S(2)}, u32[]{:S(2)}) collective-permute-start(bf16[8,128,512]{2,1,0:T(8,128)(2,1)S(1)} %convert_element_type.3.own.refs_5_), channel_id=1, source_target_pairs={{16,0},{65,1},{18,2},{67,3},{20,4},{69,5},{22,6},{71,7},{24,8},{73... | collective-permute-start | bytes 3145736 | tf_op jit(solution)/shard_map/ppermute | solution.py:49
  5.7 29.9 %collective-permute-start.3 = (bf16[8,128,512]{2,1,0:T(8,128)(2,1)S(1)}, bf16[8,128,512]{2,1,0:T(8,128)(2,1)}, u32[]{:S(2)}, u32[]{:S(2)}) collective-permute-start(bf16[8,128,512]{2,1,0:T(8,128)(2,1)S(1)} %convert_element_type.3.own.refs_5_), channel_id=1, source_target_pairs={{8,0},{33,1},{10,2},{35,3},{12,4},{37,5},{14,6},{39,7},{16,8},{41,... | collective-permute-start | bytes 3145736 | tf_op jit(solution)/shard_map/ppermute | solution.py:49
  28.8 2.4 collective-permute-start
  28.8 3.6 collective-permute-start.2
  31.2 3.9 collective-permute-start.1
  35.7 1.0 copy-start.5
  229.5 55.3 %copy-start.19 = (s32[192,5,128]{2,0,1:T(8,128)S(1)}, s32[192,5,128]{2,0,1:T(8,128)}, u32[]{:S(2)}) copy-start(s32[192,5,128]{2,0,1:T(8,128)} %param.13) | copy-start | bytes 1474564
  229.5 69.3 %collective-permute-start.7 = (bf16[16,128,512]{2,1,0:T(8,128)(2,1)}, bf16[16,128,512]{2,1,0:T(8,128)(2,1)S(1)}, u32[]{:S(2)}, u32[]{:S(2)}) collective-permute-start(bf16[16,128,512]{2,1,0:T(8,128)(2,1)} %get-tuple-element.25), channel_id=1, source_target_pairs={{32,0},{9,1},{34,2},{11,3},{36,4},{13,5},{38,6},{15,7},{40,8},{17,... | collective-permute-start | bytes 6291464 | tf_op jit(solution)/shard_map/ppermute | solution.py:49
  229.6 69.3 %collective-permute-start.8 = (bf16[16,128,512]{2,1,0:T(8,128)(2,1)}, bf16[16,128,512]{2,1,0:T(8,128)(2,1)S(1)}, u32[]{:S(2)}, u32[]{:S(2)}) collective-permute-start(bf16[16,128,512]{2,1,0:T(8,128)(2,1)} %get-tuple-element.26), channel_id=1, source_target_pairs={{96,0},{25,1},{98,2},{27,3},{100,4},{29,5},{102,6},{31,7},{104,8},... | collective-permute-start | bytes 6291464 | tf_op jit(solution)/shard_map/ppermute | solution.py:49
  232.2 88.5 %collective-permute-start.6 = (bf16[16,128,512]{2,1,0:T(8,128)(2,1)}, bf16[16,128,512]{2,1,0:T(8,128)(2,1)S(1)}, u32[]{:S(2)}, u32[]{:S(2)}) collective-permute-start(bf16[16,128,512]{2,1,0:T(8,128)(2,1)} %get-tuple-element.24), channel_id=1, source_target_pairs={{64,0},{17,1},{66,2},{19,3},{68,4},{21,5},{70,6},{23,7},{72,8},{25... | collective-permute-start | bytes 6291464 | tf_op jit(solution)/shard_map/ppermute | solution.py:49
  234.0 54.9 %copy-start.1 = (bf16[8,128,512]{2,1,0:T(8,128)(2,1)S(1)}, bf16[8,128,512]{2,1,0:T(8,128)(2,1)}, u32[]{:S(2)}) copy-start(bf16[8,128,512]{2,1,0:T(8,128)(2,1)} %copy-done) | copy-start | bytes 3145732
  234.0 54.9 %copy-start.6 = (bf16[8,128,512]{2,1,0:T(8,128)(2,1)S(1)}, bf16[8,128,512]{2,1,0:T(8,128)(2,1)}, u32[]{:S(2)}) copy-start(bf16[8,128,512]{2,1,0:T(8,128)(2,1)} %copy-done.5) | copy-start | bytes 3145732
  234.0 54.9 %copy-start.12 = (s32[276]{0:T(512)S(1)}, s32[276]{0:T(512)}, u32[]{:S(2)}) copy-start(s32[276]{0:T(512)} %get-tuple-element.19.refs_0_) | copy-start | bytes 3316
  234.0 54.9 %copy-start.13 = (s32[276]{0:T(512)S(1)}, s32[276]{0:T(512)}, u32[]{:S(2)}) copy-start(s32[276]{0:T(512)} %get-tuple-element.20.refs_1_) | copy-start | bytes 3316
  234.1 54.9 %copy-start.14 = (s32[138]{0:T(256)S(1)}, s32[138]{0:T(256)}, u32[]{:S(2)}) copy-start(s32[138]{0:T(256)} %get-tuple-element.21.refs_2_) | copy-start | bytes 1660
  234.1 54.9 %copy-start.15 = (s32[4]{0:T(128)S(1)}, s32[4]{0:T(128)}, u32[]{:S(2)}) copy-start(s32[4]{0:T(128)} %get-tuple-element.22.refs_3_) | copy-start | bytes 52
  234.1 1.3 collective-permute-start.9
  235.3 2.9 collective-permute-start.10
  238.2 4.4 collective-permute-start.11
  242.6 35.5 %collective-permute-start.12 = (f32[8,512]{1,0:T(8,128)S(1)}, f32[8,512]{1,0:T(8,128)S(1)}, u32[]{:S(2)}, u32[]{:S(2)}) collective-permute-start(f32[8,512]{1,0:T(8,128)S(1)} %add.46), channel_id=1, source_target_pairs={{0,8},{8,0},{16,24},{24,16},{1,9},{9,1},{17,25},{25,17},{2,10},{10... | collective-permute-start | bytes 49160 | tf_op jit(solution)/shard_map/ppermute | solution.py:56
  278.1 4.1 collective-permute-start.13
  282.2 2.6 collective-permute-start.14
  284.8 4.1 collective-permute-start.15
  298.9 1.3 copy-start.17
  319.4 1.3 copy-start.4
  320.8 1.3 copy-start.16
  334.6 1.3 copy-start.11
  336.0 27.2 %copy-start.2 = (bf16[8,128,512]{2,1,0:T(8,128)(2,1)}, bf16[8,128,512]{2,1,0:T(8,128)(2,1)S(1)}, u32[]{:S(2)}) copy-start(bf16[8,128,512]{2,1,0:T(8,128)(2,1)S(1)} %get-tuple-element.27.own.refs_5_) | copy-start | bytes 3145732
  336.0 26.1 %collective-permute-start.18 = (bf16[8,128,512]{2,1,0:T(8,128)(2,1)S(1)}, bf16[8,128,512]{2,1,0:T(8,128)(2,1)S(1)}, u32[]{:S(2)}, u32[]{:S(2)}) collective-permute-start(bf16[8,128,512]{2,1,0:T(8,128)(2,1)S(1)} %get-tuple-element.27.own.refs_5_), channel_id=1, source_target_pairs={{24,0},{97,1},{26,2},{99,3},{28,4},{101,5},{30,6},{103,7},{0,8},{1... | collective-permute-start | bytes 3145736 | tf_op jit(solution)/shard_map/ppermute | solution.py:49
  336.0 26.1 %collective-permute-start.17 = (bf16[8,128,512]{2,1,0:T(8,128)(2,1)S(1)}, bf16[8,128,512]{2,1,0:T(8,128)(2,1)S(1)}, u32[]{:S(2)}, u32[]{:S(2)}) collective-permute-start(bf16[8,128,512]{2,1,0:T(8,128)(2,1)S(1)} %get-tuple-element.27.own.refs_5_), channel_id=1, source_target_pairs={{16,0},{65,1},{18,2},{67,3},{20,4},{69,5},{22,6},{71,7},{24,8},{73... | collective-permute-start | bytes 3145736 | tf_op jit(solution)/shard_map/ppermute | solution.py:49
  336.0 27.1 %collective-permute-start.16 = (bf16[8,128,512]{2,1,0:T(8,128)(2,1)S(1)}, bf16[8,128,512]{2,1,0:T(8,128)(2,1)}, u32[]{:S(2)}, u32[]{:S(2)}) collective-permute-start(bf16[8,128,512]{2,1,0:T(8,128)(2,1)S(1)} %get-tuple-element.27.own.refs_5_), channel_id=1, source_target_pairs={{8,0},{33,1},{10,2},{35,3},{12,4},{37,5},{14,6},{39,7},{16,8},{41,... | collective-permute-start | bytes 3145736 | tf_op jit(solution)/shard_map/ppermute | solution.py:49
  362.1 1.4 copy-start.7
  362.1 1.0 copy-start.9
  556.3 72.4 %collective-permute-start.20 = (bf16[16,128,512]{2,1,0:T(8,128)(2,1)}, bf16[16,128,512]{2,1,0:T(8,128)(2,1)S(1)}, u32[]{:S(2)}, u32[]{:S(2)}) collective-permute-start(bf16[16,128,512]{2,1,0:T(8,128)(2,1)} %get-tuple-element.29), channel_id=1, source_target_pairs={{32,0},{9,1},{34,2},{11,3},{36,4},{13,5},{38,6},{15,7},{40,8},{17,... | collective-permute-start | bytes 6291464 | tf_op jit(solution)/shard_map/ppermute | solution.py:49
  556.4 72.3 %collective-permute-start.21 = (bf16[16,128,512]{2,1,0:T(8,128)(2,1)}, bf16[16,128,512]{2,1,0:T(8,128)(2,1)S(1)}, u32[]{:S(2)}, u32[]{:S(2)}) collective-permute-start(bf16[16,128,512]{2,1,0:T(8,128)(2,1)} %get-tuple-element.30), channel_id=1, source_target_pairs={{96,0},{25,1},{98,2},{27,3},{100,4},{29,5},{102,6},{31,7},{104,8},... | collective-permute-start | bytes 6291464 | tf_op jit(solution)/shard_map/ppermute | solution.py:49
  559.0 90.2 %collective-permute-start.19 = (bf16[16,128,512]{2,1,0:T(8,128)(2,1)}, bf16[16,128,512]{2,1,0:T(8,128)(2,1)S(1)}, u32[]{:S(2)}, u32[]{:S(2)}) collective-permute-start(bf16[16,128,512]{2,1,0:T(8,128)(2,1)} %get-tuple-element.28), channel_id=1, source_target_pairs={{64,0},{17,1},{66,2},{19,3},{68,4},{21,5},{70,6},{23,7},{72,8},{25... | collective-permute-start | bytes 6291464 | tf_op jit(solution)/shard_map/ppermute | solution.py:49
  559.0 1.2 collective-permute-start.22
  560.2 2.9 collective-permute-start.23
  563.1 4.4 collective-permute-start.24
  567.5 37.1 %collective-permute-start.25 = (f32[8,512]{1,0:T(8,128)S(1)}, f32[8,512]{1,0:T(8,128)S(1)}, u32[]{:S(2)}, u32[]{:S(2)}) collective-permute-start(f32[8,512]{1,0:T(8,128)S(1)} %add.53), channel_id=1, source_target_pairs={{0,8},{8,0},{16,24},{24,16},{1,9},{9,1},{17,25},{25,17},{2,10},{10... | collective-permute-start | bytes 49160 | tf_op jit(solution)/shard_map/ppermute | solution.py:56
  604.6 4.1 collective-permute-start.26
  608.7 2.6 collective-permute-start.27
  611.3 4.1 collective-permute-start.28
  615.4 1.2 copy-start.3
  616.6 1.2 copy-start.8
  617.8 1.2 copy-start.10
  628.7 1.3 copy-start.18
